TPU v7x, 32 devices: a whole 2x2x4 slice. The times are simulated.
32 devices in a mesh: src: 4 (over z), space: 8 (over y, x, core).
Axes of the slice: x: 2, y: 2, z: 4, core: 2. Of those that a mesh axis runs over, the one named last changes fastest.
Arguments:
- background: float32 [2, 4, 3, 16, 32, 128], P(None, 'src', None, 'space'), may hold values from -6 to 6
- warm_start: float32 [2, 4, 3, 16, 32, 128], P(None, 'src', None, 'space'), may hold values from -0.15625 to 0.15625
- conductivity: float32 [16, 32, 128], P('space'), may hold values from 0.3 to 3
- frequencies: float32 [8], replicated, may hold values from 0.1 to 1
- pair_freq: int32 [4], P('src'), may hold values from 0 to 7
- weighted_residual: float32 [2, 4, 1024], P(None, 'src', 'space'), may hold values from -6 to 6
- datum_layer_index: int32 [1024, 1], replicated, may hold values from 0 to 7; in each aligned block of 128 rows (0 to 127, 128 to 255, ...) at most 32 rows name the same one
- receiver_flat_cell: int32 [1024], replicated, may hold values from 0 to 8191
- receiver_component: int32 [1024], replicated, may hold values from 0 to 2
Outputs:
- adjoint: float32 [2, 4, 3, 16, 32, 128], P(None, 'src', None, 'space')
- gradient: float32 [16, 32, 128], P('space', 'src')
Inputs may be any that keep to these rules, and one draw needn't show every extreme that they name: `datum_layer_index`: among the 128 measurements of each aligned block (the measurements of one device), no slab is named by more than 32 of them, a bound that some block reaches.
All inputs are finite; a program needn't handle non-finite values.
Results may differ from a plain program's by a relative error of at most 0.0001.
Values sent between devices are 32-bit elements; how exact they have to be, the bound alone decides.
A program may use at most 64 MiB of HBM per device.

v0:
```python
import jax
import jax.numpy as jnp
from jax import lax
from jax.sharding import PartitionSpec as P

ITERS = 4


def from_behind(block, axis, distance):
    devices = range(lax.axis_size(axis))
    route = [(i - distance, i) for i in devices if i - distance in devices]
    return lax.ppermute(block, axis, route)


def diff_forward(field, spatial):
    base = field[..., :-1, :-1, :-1]
    if spatial == 0:
        return field[..., 1:, :-1, :-1] - base
    if spatial == 1:
        return field[..., :-1, 1:, :-1] - base
    return field[..., :-1, :-1, 1:] - base


def diff_backward(field, spatial):
    base = field[..., 1:, 1:, 1:]
    if spatial == 0:
        return base - field[..., :-1, 1:, 1:]
    if spatial == 1:
        return base - field[..., 1:, :-1, 1:]
    return base - field[..., 1:, 1:, :-1]


def curl_forward(padded):
    comp_x = padded[..., 0, :, :, :]
    comp_y = padded[..., 1, :, :, :]
    comp_z = padded[..., 2, :, :, :]
    mag_x = diff_forward(comp_z, 1) - diff_forward(comp_y, 2)
    mag_y = diff_forward(comp_x, 2) - diff_forward(comp_z, 0)
    mag_z = diff_forward(comp_y, 0) - diff_forward(comp_x, 1)
    return jnp.stack([mag_x, mag_y, mag_z], axis=-4)


def curl_backward(magnetic):
    mag_x = magnetic[..., 0, :, :, :]
    mag_y = magnetic[..., 1, :, :, :]
    mag_z = magnetic[..., 2, :, :, :]
    out_x = diff_backward(mag_z, 1) - diff_backward(mag_y, 2)
    out_y = diff_backward(mag_x, 2) - diff_backward(mag_z, 0)
    out_z = diff_backward(mag_y, 0) - diff_backward(mag_x, 1)
    return jnp.stack([out_x, out_y, out_z], axis=-4)


def pad_sides(field):
    return jnp.pad(field, ((0, 0), (0, 0), (0, 0), (0, 0), (1, 1), (1, 1)))


def curl_curl(field, measurement_position):
    upper = from_behind(field[:, :, :, 0:1], "space", -1)
    extended = jnp.concatenate([jnp.zeros_like(upper), field, upper], axis=3)
    magnetic = curl_forward(pad_sides(extended))
    lower = from_behind(magnetic[:, :, :, -1:], "space", 1)
    first_plane = jnp.where(measurement_position == 0, magnetic[:, :, :, 0:1], lower)
    magnetic = jnp.concatenate([first_plane, magnetic[:, :, :, 1:]], axis=3)
    return curl_backward(magnetic)


def inner(first_vec, second_vec):
    real_part = jnp.sum(
        first_vec[0] * second_vec[0] + first_vec[1] * second_vec[1], axis=(1, 2, 3, 4)
    )
    quadrature_share = jnp.sum(
        first_vec[0] * second_vec[1] - first_vec[1] * second_vec[0], axis=(1, 2, 3, 4)
    )
    return (real_part, quadrature_share)


def squared(field):
    return jnp.sum(field[0] * field[0] + field[1] * field[1], axis=(1, 2, 3, 4))


def scaled(coef_re, coef_im, field):
    part_re = coef_re[:, None, None, None, None]
    part_im = coef_im[:, None, None, None, None]
    return jnp.stack(
        [part_re * field[0] - part_im * field[1], part_re * field[1] + part_im * field[0]]
    )


def shards(
    background,
    warm_start,
    conductivity,
    frequencies,
    pair_freq,
    weighted_residual,
    datum_layer_index,
    receiver_flat_cell,
    receiver_component,
):
    slab_partition = lax.axis_size("space")
    measurement_position = lax.axis_index("space")
    pair_count = background.shape[1]
    planes, rows_y, rows_z = (background.shape[3], background.shape[4], background.shape[5])
    slab_cells = planes * rows_y * rows_z
    local_measurements = weighted_residual.shape[2]
    slab_limit = 2 * local_measurements // slab_partition
    owning_slab = datum_layer_index[:, 0]
    holding_slab = lax.dynamic_slice_in_dim(
        owning_slab, measurement_position * local_measurements, local_measurements
    )
    one_hot = (
        holding_slab[:, None] == jnp.arange(slab_partition, dtype=jnp.int32)[None, :]
    ).astype(jnp.int32)
    rank_in = jnp.sum(jnp.cumsum(one_hot, axis=0) * one_hot, axis=1) - 1
    target_layer_slot = holding_slab * slab_limit + rank_in
    outgoing = (
        jnp.zeros((2, pair_count, slab_partition * slab_limit), jnp.float32)
        .at[:, :, target_layer_slot]
        .set(weighted_residual)
    )
    incoming = lax.all_to_all(outgoing, "space", split_axis=2, concat_axis=2, tiled=True)
    slab_blocks = owning_slab.reshape(slab_partition, local_measurements)
    is_mine = (slab_blocks == measurement_position).astype(jnp.int32)
    slot_index = (
        jnp.cumsum(is_mine, axis=1)
        - 1
        + jnp.arange(slab_partition, dtype=jnp.int32)[:, None] * slab_limit
    )
    slot_index = jnp.where(is_mine > 0, slot_index, 0).reshape(-1)
    values = incoming[:, :, slot_index] * is_mine.reshape(-1).astype(jnp.float32)
    target = receiver_component * slab_cells + receiver_flat_cell
    flat_src = jnp.zeros((2, pair_count, 3 * slab_cells), jnp.float32).at[:, :, target].add(values)
    source = flat_src.reshape(2, pair_count, 3, planes, rows_y, rows_z)
    freq_hot = (
        pair_freq[:, None] == jnp.arange(frequencies.shape[0], dtype=jnp.int32)[None, :]
    ).astype(jnp.float32)
    wave_k = jnp.sum(freq_hot * frequencies[None, :], axis=1)
    damping = wave_k[:, None, None, None, None] * conductivity[None, None]

    def operate(field):
        curled = curl_curl(field, measurement_position)
        return jnp.stack([curled[0] - damping * field[1], curled[1] + damping * field[0]])

    adjoint = warm_start
    residual = source - operate(adjoint)
    direction = residual
    mapped = operate(direction)
    mixed_product_real, cross_im = inner(mapped, residual)
    mixed_product_real, cross_im, projected_magnitude = lax.psum(
        (mixed_product_real, cross_im, squared(mapped)), "space"
    )
    for sweep in range(ITERS):
        alpha_re = mixed_product_real / projected_magnitude
        alpha_im = cross_im / projected_magnitude
        adjoint = adjoint + scaled(alpha_re, alpha_im, direction)
        residual = residual - scaled(alpha_re, alpha_im, mapped)
        if sweep + 1 < ITERS:
            fresh = operate(residual)
            fresh_re, fresh_im = inner(fresh, residual)
            turn_re, turn_im = inner(mapped, fresh)
            fresh_re, fresh_im, fresh_norm, turn_re, turn_im = lax.psum(
                (fresh_re, fresh_im, squared(fresh), turn_re, turn_im), "space"
            )
            beta_re = -turn_re / projected_magnitude
            beta_im = -turn_im / projected_magnitude
            left_re = mixed_product_real - alpha_re * projected_magnitude
            left_im = cross_im - alpha_im * projected_magnitude
            mixed_product_real = fresh_re + beta_re * left_re + beta_im * left_im
            cross_im = fresh_im + beta_re * left_im - beta_im * left_re
            projected_magnitude = (
                fresh_norm
                + 2.0 * (beta_re * turn_re + beta_im * turn_im)
                + (beta_re * beta_re + beta_im * beta_im) * projected_magnitude
            )
            direction = residual + scaled(beta_re, beta_im, direction)
            mapped = fresh + scaled(beta_re, beta_im, mapped)
    weights = wave_k[:, None, None, None, None]
    local_terms = jnp.sum(
        weights * (adjoint[0] * background[1] + adjoint[1] * background[0]), axis=(0, 1)
    )
    gradient = lax.psum_scatter(local_terms, "src", scatter_dimension=1, tiled=True)
    return (adjoint, gradient)


def solution(mesh):
    placed = (
        P(None, "src", None, "space", None, None),
        P(None, "src", None, "space", None, None),
        P("space", None, None),
        P(),
        P("src"),
        P(None, "src", "space"),
        P(),
        P(),
        P(),
    )
    return jax.shard_map(
        shards,
        mesh=mesh,
        in_specs=placed,
        out_specs=(P(None, "src", None, "space", None, None), P("space", "src", None)),
        check_vma=False,
    )
```

profile of v0, /device:TPU:0, one launch (start us, length us, event | category | flops | bytes accessed | tf_op | source)
XLA Modules:
  0.0 210.2 jit_solution(1392780173967309575)
XLA Ops:
  7.2 0.7 fusion.149
  8.3 0.7 fusion.148
  8.9 0.8 copy.49
  9.7 1.5 scatter_custom_fusion
  11.2 5.2 %all-to-all-start = ((f32[2,1,256]{0,1,2:T(1,128)}), f32[2,1,256]{0,1,2:T(1,128)S(1)}, u32[]{:S(2)}, u32[]{:S(2)}) async-start(f32[2,1,256]{0,1,2:T(1,128)} %bitcast.6), calls=%async_computation | async-start | bytes 262144 | tf_op jit(solution)/shard_map/all_to_all | solution.py:121
  16.5 0.9 slice.782
  17.4 1.3 collective-permute-start
  18.7 0.7 fusion.155
  19.4 0.3 reduce_window_sum.23
  20.4 1.3 fusion.147
  21.7 1.4 broadcast_multiply_fusion
  23.1 1.0 pad_maximum_fusion.5
  24.1 0.3 fusion.3
  24.4 0.2 fusion.73
  24.7 3.0 %collective-permute-start.1 = (f32[2,1,3,1,33,129]{5,4,3,0,2,1:T(8,128)S(1)}, f32[2,1,3,1,33,129]{5,4,3,0,2,1:T(8,128)S(1)}, u32[]{:S(2)}, u32[]{:S(2)}) collective-permute-start(f32[2,1,3,1,33,129]{5,4,3,0,2,1:T(8,128)S(1)} %slice.793), channel_id=1, source_target_pairs={{0,1},{1,2},{2,3},{3,4},{4,5},{5,6},{6,7},{8,9},{9,10},{10,11},{11... | collective-permute-start | bytes 306512 | tf_op jit(solution)/shard_map/ppermute | solution.py:12
  27.8 0.7 compare_select_fusion.2
  28.5 14.6 %scatter_custom_fusion.1 = f32[2,24576]{0,1:T(8,128)} fusion(s32[1024]{0:T(1024)S(1)} %get-tuple-element.150, f32[]{:T(128)} %constant.13.clone.1, f32[1024]{0:T(1024)S(1)} %bitcast.402, f32[2,256]{0,1:T(8,128)S(1)} %bitcast.400, s32[1024]{0:T(1024)S(1)} %get-tuple-element.151), kind=kCustom, calls=%fused_computation.3 | custom fusion | flops 4096 | bytes 335876 | tf_op jit(solution)/shard_map/scatter-add | solution.py:132
  43.1 7.6 %copy.57 = f32[2,1,3,2,32,128]{5,4,3,0,2,1:T(8,128)S(1)} copy(f32[2,1,3,2,32,128]{0,5,4,3,2,1:T(8,128)} %bitcast.399) | data formatting | bytes 393216 | tf_op jit(solution)/shard_map/reshape | solution.py:133
  51.2 1.3 collective-permute-start.2
  52.5 3.1 %collective-permute-done.2 = f32[2,1,3,1,32,128]{5,4,3,0,2,1:T(8,128)S(1)} collective-permute-done((f32[2,1,3,1,32,128]{5,4,3,0,2,1:T(8,128)S(1)}, f32[2,1,3,1,32,128]{5,4,3,0,2,1:T(8,128)S(1)}, u32[]{:S(2)}, u32[]{:S(2)}) %collective-permute-start.2) | collective-permute-done | bytes 98336 | tf_op jit(solution)/shard_map/ppermute | solution.py:12
  55.7 0.3 fusion.6
  56.0 0.2 fusion.66
  56.3 5.2 %collective-permute-start.3 = (f32[2,1,3,1,33,129]{5,4,3,0,2,1:T(8,128)S(1)}, f32[2,1,3,1,33,129]{5,4,3,0,2,1:T(8,128)S(1)}, u32[]{:S(2)}, u32[]{:S(2)}) collective-permute-start(f32[2,1,3,1,33,129]{5,4,3,0,2,1:T(8,128)S(1)} %slice.823), channel_id=1, source_target_pairs={{0,1},{1,2},{2,3},{3,4},{4,5},{5,6},{6,7},{8,9},{9,10},{10,11},{11... | collective-permute-start | bytes 306512 | tf_op jit(solution)/shard_map/ppermute | solution.py:12
  61.5 1.1 collective-permute-done.3
  62.9 0.7 fusion.88
  63.5 15.0 %all-reduce.8 = (f32[1]{0:T(128)}, f32[1]{0:T(128)}, f32[1]{0:T(128)}) all-reduce(f32[1]{0:T(128)} %bitcast.51, f32[1]{0:T(128)} %bitcast.48, f32[1]{0:T(128)} %bitcast.47), channel_id=1, replica_groups=mesh['src'=4,'space'=8] {'space'}, use_global_device_ids=true, to_apply=%region_11.12 | all-reduce | flops 3 | bytes 24 | tf_op jit(solution)/shard_map/psum | solution.py:149
  81.5 1.3 collective-permute-start.4
  82.8 1.9 collective-permute-done.4
  84.8 0.3 fusion.9
  85.4 5.6 %collective-permute-start.5 = (f32[2,1,3,1,33,129]{5,4,3,0,2,1:T(8,128)S(1)}, f32[2,1,3,1,33,129]{5,4,3,0,2,1:T(8,128)S(1)}, u32[]{:S(2)}, u32[]{:S(2)}) collective-permute-start(f32[2,1,3,1,33,129]{5,4,3,0,2,1:T(8,128)S(1)} %slice.853), channel_id=1, source_target_pairs={{0,1},{1,2},{2,3},{3,4},{4,5},{5,6},{6,7},{8,9},{9,10},{10,11},{11... | collective-permute-start | bytes 306512 | tf_op jit(solution)/shard_map/ppermute | solution.py:12
  94.1 0.7 fusion.110
  94.8 15.3 %all-reduce.7 = (f32[1]{0:T(128)}, f32[1]{0:T(128)}, f32[1]{0:T(128)}, f32[1]{0:T(128)}, f32[1]{0:T(128)}) all-reduce(f32[1]{0:T(128)} %bitcast.74, f32[1]{0:T(128)} %bitcast.73, f32[1]{0:T(128)} %bitcast.80, f32[1]{0:T(128)} %bitcast.75, f32[1]{0:T(128)} %bitcast.72), channel_id=1, replica_groups=mesh['src'=4,'space'=8] {'space'}, use_global_device_ids=true, to_apply=%region_17.18 | all-reduce | flops 5 | bytes 40 | tf_op jit(solution)/shard_map/psum | solution.py:161
  117.1 1.3 collective-permute-start.6
  118.4 1.9 collective-permute-done.6
  120.4 0.3 fusion.12
  121.0 5.0 %collective-permute-start.7 = (f32[2,1,3,1,33,129]{5,4,3,0,2,1:T(8,128)S(1)}, f32[2,1,3,1,33,129]{5,4,3,0,2,1:T(8,128)S(1)}, u32[]{:S(2)}, u32[]{:S(2)}) collective-permute-start(f32[2,1,3,1,33,129]{5,4,3,0,2,1:T(8,128)S(1)} %slice.887), channel_id=1, source_target_pairs={{0,1},{1,2},{2,3},{3,4},{4,5},{5,6},{6,7},{8,9},{9,10},{10,11},{11... | collective-permute-start | bytes 306512 | tf_op jit(solution)/shard_map/ppermute | solution.py:12
  126.1 1.0 collective-permute-done.7
  127.5 0.8 fusion.102
  128.3 16.0 %all-reduce.6 = (f32[1]{0:T(128)}, f32[1]{0:T(128)}, f32[1]{0:T(128)}, f32[1]{0:T(128)}, f32[1]{0:T(128)}) all-reduce(f32[1]{0:T(128)} %bitcast.107, f32[1]{0:T(128)} %bitcast.106, f32[1]{0:T(128)} %bitcast.112, f32[1]{0:T(128)} %bitcast.108, f32[1]{0:T(128)} %bitcast.103), channel_id=1, replica_groups=mesh['src'=4,'space'=8] {'space'}, use_global_device_ids=true, to_apply=%region_27.28 | all-reduce | flops 5 | bytes 40 | tf_op jit(solution)/shard_map/psum | solution.py:161
  149.1 1.3 collective-permute-start.8
  150.4 1.9 collective-permute-done.8
  152.4 0.3 fusion.15
  153.0 5.0 %collective-permute-start.9 = (f32[2,1,3,1,33,129]{5,4,3,0,2,1:T(8,128)S(1)}, f32[2,1,3,1,33,129]{5,4,3,0,2,1:T(8,128)S(1)}, u32[]{:S(2)}, u32[]{:S(2)}) collective-permute-start(f32[2,1,3,1,33,129]{5,4,3,0,2,1:T(8,128)S(1)} %slice.921), channel_id=1, source_target_pairs={{0,1},{1,2},{2,3},{3,4},{4,5},{5,6},{6,7},{8,9},{9,10},{10,11},{11... | collective-permute-start | bytes 306512 | tf_op jit(solution)/shard_map/ppermute | solution.py:12
  158.1 1.0 collective-permute-done.9
  159.5 0.8 add_reduce_fusion.1
  160.2 15.9 %all-reduce.5 = (f32[1]{0:T(128)}, f32[1]{0:T(128)}, f32[1]{0:T(128)}, f32[1]{0:T(128)}, f32[1]{0:T(128)}) all-reduce(f32[1]{0:T(128)} %bitcast.136, f32[1]{0:T(128)} %bitcast.135, f32[1]{0:T(128)} %bitcast.141, f32[1]{0:T(128)} %bitcast.137, f32[1]{0:T(128)} %bitcast.132), channel_id=1, replica_groups=mesh['src'=4,'space'=8] {'space'}, use_global_device_ids=true, to_apply=%region_37.38 | all-reduce | flops 5 | bytes 40 | tf_op jit(solution)/shard_map/psum | solution.py:161
  180.8 1.2 fusion.84
  182.1 21.2 %reduce-scatter.2.cloned.1.call-done = f32[2,8,128]{2,1,0:T(8,128)} async-done(((f32[2,32,128]{2,1,0:T(8,128)}), f32[2,8,128]{2,1,0:T(8,128)}) %reduce-scatter.2.cloned.1.call-update) | async-done | bytes 8208 | tf_op jit(solution)/shard_map/reduce_scatter | solution.py:181
  (93 shorter events, 4.6 us)
Async XLA Ops:
  11.2 17.3 %all-to-all-start = ((f32[2,1,256]{0,1,2:T(1,128)}), f32[2,1,256]{0,1,2:T(1,128)S(1)}, u32[]{:S(2)}, u32[]{:S(2)}) async-start(f32[2,1,256]{0,1,2:T(1,128)} %bitcast.6), calls=%async_computation | async-start | bytes 262144 | tf_op jit(solution)/shard_map/all_to_all | solution.py:121
  16.4 186.9 %reduce-scatter.2.cloned.1.call-start = ((), (), s32[]{:S(2)}) async-start(), calls=%async_computation.2 | async-start | bytes 40960 | tf_op jit(solution)/shard_map/reduce_scatter | solution.py:181
  17.4 5.7 %collective-permute-start = (f32[2,1,3,1,32,128]{5,4,3,0,2,1:T(8,128)S(1)}, f32[2,1,3,1,32,128]{5,4,3,0,2,1:T(8,128)S(1)}, u32[]{:S(2)}, u32[]{:S(2)}) collective-permute-start(f32[2,1,3,1,32,128]{5,4,3,0,2,1:T(8,128)S(1)} %copy.109), channel_id=1, source_target_pairs={{1,0},{2,1},{3,2},{4,3},{5,4},{6,5},{7,6},{9,8},{10,9},{11,10},{12... | collective-permute-start | bytes 294920 | tf_op jit(solution)/shard_map/ppermute | solution.py:12
  24.7 26.0 %collective-permute-start.1 = (f32[2,1,3,1,33,129]{5,4,3,0,2,1:T(8,128)S(1)}, f32[2,1,3,1,33,129]{5,4,3,0,2,1:T(8,128)S(1)}, u32[]{:S(2)}, u32[]{:S(2)}) collective-permute-start(f32[2,1,3,1,33,129]{5,4,3,0,2,1:T(8,128)S(1)} %slice.793), channel_id=1, source_target_pairs={{0,1},{1,2},{2,3},{3,4},{4,5},{5,6},{6,7},{8,9},{9,10},{10,11},{11... | collective-permute-start | bytes 306512 | tf_op jit(solution)/shard_map/ppermute | solution.py:12
  28.5 22.6 %copy-start = (f32[2,1,3,2,32,128]{5,4,3,2,1,0:T(8,128)S(1)}, f32[2,1,3,2,32,128]{5,4,3,2,1,0:T(8,128)}, u32[]{:S(2)}) copy-start(f32[2,1,3,2,32,128]{5,4,3,2,1,0:T(8,128)} %param.10) | copy-start | bytes 589828
  51.2 4.4 %collective-permute-start.2 = (f32[2,1,3,1,32,128]{5,4,3,0,2,1:T(8,128)S(1)}, f32[2,1,3,1,32,128]{5,4,3,0,2,1:T(8,128)S(1)}, u32[]{:S(2)}, u32[]{:S(2)}) collective-permute-start(f32[2,1,3,1,32,128]{5,4,3,0,2,1:T(8,128)S(1)} %slice.812), channel_id=1, source_target_pairs={{1,0},{2,1},{3,2},{4,3},{5,4},{6,5},{7,6},{9,8},{10,9},{11,10},{12... | collective-permute-start | bytes 294920 | tf_op jit(solution)/shard_map/ppermute | solution.py:12
  56.3 6.3 %collective-permute-start.3 = (f32[2,1,3,1,33,129]{5,4,3,0,2,1:T(8,128)S(1)}, f32[2,1,3,1,33,129]{5,4,3,0,2,1:T(8,128)S(1)}, u32[]{:S(2)}, u32[]{:S(2)}) collective-permute-start(f32[2,1,3,1,33,129]{5,4,3,0,2,1:T(8,128)S(1)} %slice.823), channel_id=1, source_target_pairs={{0,1},{1,2},{2,3},{3,4},{4,5},{5,6},{6,7},{8,9},{9,10},{10,11},{11... | collective-permute-start | bytes 306512 | tf_op jit(solution)/shard_map/ppermute | solution.py:12
  81.5 3.2 %collective-permute-start.4 = (f32[2,1,3,1,32,128]{5,4,3,0,2,1:T(8,128)S(1)}, f32[2,1,3,1,32,128]{5,4,3,0,2,1:T(8,128)S(1)}, u32[]{:S(2)}, u32[]{:S(2)}) collective-permute-start(f32[2,1,3,1,32,128]{5,4,3,0,2,1:T(8,128)S(1)} %slice.842), channel_id=1, source_target_pairs={{1,0},{2,1},{3,2},{4,3},{5,4},{6,5},{7,6},{9,8},{10,9},{11,10},{12... | collective-permute-start | bytes 294920 | tf_op jit(solution)/shard_map/ppermute | solution.py:12
  85.4 8.3 %collective-permute-start.5 = (f32[2,1,3,1,33,129]{5,4,3,0,2,1:T(8,128)S(1)}, f32[2,1,3,1,33,129]{5,4,3,0,2,1:T(8,128)S(1)}, u32[]{:S(2)}, u32[]{:S(2)}) collective-permute-start(f32[2,1,3,1,33,129]{5,4,3,0,2,1:T(8,128)S(1)} %slice.853), channel_id=1, source_target_pairs={{0,1},{1,2},{2,3},{3,4},{4,5},{5,6},{6,7},{8,9},{9,10},{10,11},{11... | collective-permute-start | bytes 306512 | tf_op jit(solution)/shard_map/ppermute | solution.py:12
  117.1 3.2 %collective-permute-start.6 = (f32[2,1,3,1,32,128]{5,4,3,0,2,1:T(8,128)S(1)}, f32[2,1,3,1,32,128]{5,4,3,0,2,1:T(8,128)S(1)}, u32[]{:S(2)}, u32[]{:S(2)}) collective-permute-start(f32[2,1,3,1,32,128]{5,4,3,0,2,1:T(8,128)S(1)} %slice.876), channel_id=1, source_target_pairs={{1,0},{2,1},{3,2},{4,3},{5,4},{6,5},{7,6},{9,8},{10,9},{11,10},{12... | collective-permute-start | bytes 294920 | tf_op jit(solution)/shard_map/ppermute | solution.py:12
  121.0 6.1 %collective-permute-start.7 = (f32[2,1,3,1,33,129]{5,4,3,0,2,1:T(8,128)S(1)}, f32[2,1,3,1,33,129]{5,4,3,0,2,1:T(8,128)S(1)}, u32[]{:S(2)}, u32[]{:S(2)}) collective-permute-start(f32[2,1,3,1,33,129]{5,4,3,0,2,1:T(8,128)S(1)} %slice.887), channel_id=1, source_target_pairs={{0,1},{1,2},{2,3},{3,4},{4,5},{5,6},{6,7},{8,9},{9,10},{10,11},{11... | collective-permute-start | bytes 306512 | tf_op jit(solution)/shard_map/ppermute | solution.py:12
  126.0 54.8 %copy-start.2 = (f32[2,1,3,2,32,128]{5,4,3,2,1,0:T(8,128)S(1)}, f32[2,1,3,2,32,128]{5,4,3,2,1,0:T(8,128)}, u32[]{:S(2)}) copy-start(f32[2,1,3,2,32,128]{5,4,3,2,1,0:T(8,128)} %param.9) | copy-start | bytes 589828
  149.1 3.2 %collective-permute-start.8 = (f32[2,1,3,1,32,128]{5,4,3,0,2,1:T(8,128)S(1)}, f32[2,1,3,1,32,128]{5,4,3,0,2,1:T(8,128)S(1)}, u32[]{:S(2)}, u32[]{:S(2)}) collective-permute-start(f32[2,1,3,1,32,128]{5,4,3,0,2,1:T(8,128)S(1)} %slice.910), channel_id=1, source_target_pairs={{1,0},{2,1},{3,2},{4,3},{5,4},{6,5},{7,6},{9,8},{10,9},{11,10},{12... | collective-permute-start | bytes 294920 | tf_op jit(solution)/shard_map/ppermute | solution.py:12
  153.0 6.1 %collective-permute-start.9 = (f32[2,1,3,1,33,129]{5,4,3,0,2,1:T(8,128)S(1)}, f32[2,1,3,1,33,129]{5,4,3,0,2,1:T(8,128)S(1)}, u32[]{:S(2)}, u32[]{:S(2)}) collective-permute-start(f32[2,1,3,1,33,129]{5,4,3,0,2,1:T(8,128)S(1)} %slice.921), channel_id=1, source_target_pairs={{0,1},{1,2},{2,3},{3,4},{4,5},{5,6},{6,7},{8,9},{9,10},{10,11},{11... | collective-permute-start | bytes 306512 | tf_op jit(solution)/shard_map/ppermute | solution.py:12
  180.8 22.5 %copy-start.1 = (f32[2,1,3,2,32,128]{5,4,3,2,1,0:T(8,128)}, f32[2,1,3,2,32,128]{5,4,3,2,1,0:T(8,128)S(1)}, u32[]{:S(2)}) copy-start(f32[2,1,3,2,32,128]{5,4,3,2,1,0:T(8,128)S(1)} %fusion.75) | copy-start | bytes 589828
Sparse Core Ops, SparseCore 0:
  182.2 21.0 reduce-scatter.1
where the time goes:
time: 211 us; the launch traced here: 210 us
  blocking collectives  62.3 us (30%)
  between operations  36.6 us (17%)
  starting transfers between devices  35.5 us (17%)
  waiting for transfers between devices  33.2 us (16%)
  other arithmetic  29.3 us (14%)
  local copies, waits for them, and re-layouts  13.4 us (6%)
    psum x3, blocking collectives, shards(): lax.psum((fresh_re, fresh_im, squared(fresh), turn_re, turn_im), 'space')  47.2 us
    ppermute x10, starting transfers between devices, from_behind(): return lax.ppermute(block, axis, route)  30.2 us
    reduce_scatter x1, waiting for transfers between devices, shards(): lax.psum_scatter(local_terms, 'src', scatter_dimension=1, tiled=True)  21.2 us
    psum x1, blocking collectives, shards(): lax.psum((mixed_product_real, cross_im, squared(mapped)), 'space')  15 us
    scatter-add x1, other arithmetic, shards(): jnp.zeros((2, pair_count, 3 * slab_cells), jnp.float32).at[:, :, target]  14.6 us
    ppermute x10, waiting for transfers between devices, from_behind(): return lax.ppermute(block, axis, route)  11.9 us
    reshape x1, local copies, waits for them, and re-layouts, shards(): source = flat_src.reshape(2, pair_count, 3, planes, rows_y, rows_z)  7.59 us
    all_to_all x1, starting transfers between devices, shards(): lax.all_to_all(outgoing, 'space', split_axis=2, concat_axis=2, tiled=True)  5.2 us
  transfers between devices with their start and end apart: 12, of which 8 were waited for; matrix products, arithmetic and copies ran while one was open for 14% of the time, Pallas kernels for 0%

commit v1 on v0

v1 whole, which is shorter than its diff:
```python
import functools

import jax
import jax.numpy as jnp
from jax import lax
from jax.experimental import pallas as pl
from jax.experimental.pallas import tpu as pltpu
from jax.sharding import PartitionSpec as P

ITERS = 4
SHIFT = 6.0
MESH = pl.DeviceIdType.MESH


def up(field, axis):
    length = field.shape[axis]
    cell = lax.broadcasted_iota(jnp.int32, field.shape, axis)
    return jnp.where(cell == length - 1, 0.0, pltpu.roll(field, length - 1, axis))


def down(field, axis, first):
    cell = lax.broadcasted_iota(jnp.int32, field.shape, axis)
    return jnp.where(cell == 0, first, pltpu.roll(field, 1, axis))


def edge_sums(comp_x, comp_y, comp_z):
    return comp_y + (up(comp_x, 1) - comp_x), comp_z + (up(comp_x, 2) - comp_x)


def curl_curl(comp_x, comp_y, comp_z):
    zero = jnp.zeros_like(comp_x[:1])
    sum_y, sum_z = edge_sums(comp_x, comp_y, comp_z)
    mag_z = jnp.concatenate([comp_y[1:], zero]) - sum_y
    mag_y = sum_z - jnp.concatenate([comp_z[1:], zero])
    mag_x = (up(comp_z, 1) - comp_z) - (up(comp_y, 2) - comp_y)
    before_z = jnp.concatenate([comp_y[:1], mag_z[:-1]])
    before_y = jnp.concatenate([-comp_z[:1], mag_y[:-1]])
    out_x = (mag_z - down(mag_z, 1, -comp_x)) - (mag_y - down(mag_y, 2, comp_x))
    out_y = (mag_x - down(mag_x, 2, -comp_y)) - (mag_z - before_z)
    out_z = (mag_y - before_y) - (mag_x - down(mag_x, 1, comp_z))
    return out_x, out_y, out_z


def c_mul(a, b):
    return a[0] * b[0] - a[1] * b[1], a[0] * b[1] + a[1] * b[0]


def c_add(a, b):
    return a[0] + b[0], a[1] + b[1]


def c_sum(terms):
    total = terms[0]
    for term in terms[1:]:
        total = c_add(total, term)
    return total


def gram_slots():
    slots = {}
    for k in range(ITERS + 1):
        for j in range(k + 1):
            slots[j, k, 0] = len(slots)
            if j < k:
                slots[j, k, 1] = len(slots)
    return slots


def combination(gram):
    zero = jnp.zeros_like(gram(0, 0)[0])
    one = zero + 1.0

    def dot(left, right):
        return c_sum([c_mul(a, b) for a, b in zip(left, right)])

    def operate(vec):
        shifted = [(SHIFT * a, SHIFT * b) for a, b in vec] + [(zero, zero)]
        return [shifted[0]] + [c_add(s, v) for s, v in zip(shifted[1:], vec)]

    def axpy(coef, vec, base):
        base = list(base) + [(zero, zero)] * (len(vec) - len(base))
        moved = [c_add(b, c_mul(coef, v)) for v, b in zip(vec, base)]
        return moved + base[len(vec):]

    residual = [(one, zero)]
    direction = residual
    mapped = operate(direction)
    update = [(zero, zero)]
    for sweep in range(ITERS):
        weights = [
            c_sum([c_mul((m[0], -m[1]), gram(j, k)) for j, m in enumerate(mapped)])
            for k in range(min(len(mapped) + 1, ITERS + 1))
        ]
        norm = dot(weights[: len(mapped)], mapped)[0]
        mixed = dot(weights, residual)
        alpha = (mixed[0] / norm, mixed[1] / norm)
        update = axpy(alpha, direction, update)
        if sweep + 1 < ITERS:
            residual = axpy((-alpha[0], -alpha[1]), mapped, residual)
            fresh = operate(residual)
            turn = dot(weights, fresh)
            beta = (-turn[0] / norm, -turn[1] / norm)
            direction = axpy(beta, direction, residual)
            mapped = axpy(beta, mapped, fresh)
    return update


def kernel(
    n_space,
    n_src,
    background,
    warm,
    conductivity,
    frequencies,
    pair_freq,
    measured,
    layer,
    cell,
    component,
    adjoint,
    gradient,
    basis,
    sums,
    above,
    below,
    source,
    measured_all,
    gram_rows,
    gram_all,
    shares,
    shares_in,
    halo_send,
    halo_recv,
    measured_send,
    measured_recv,
    gram_send,
    gram_recv,
    share_send,
    share_recv,
):
    me = lax.axis_index("space")
    pair = lax.axis_index("src")
    planes, rows_y, rows_z = conductivity.shape
    last = planes - 1

    barrier = pltpu.get_barrier_semaphore()
    for off in range(1, n_space):
        pl.semaphore_signal(
            barrier, 1, device_id={"space": lax.rem(me + off, n_space)}, device_id_type=MESH
        )
    for off in range(1, n_src):
        pl.semaphore_signal(
            barrier, 1, device_id={"src": lax.rem(pair + off, n_src)}, device_id_type=MESH
        )

    wave_k = frequencies[pair_freq[0]]

    def store_sums(field):
        for part in range(2):
            sum_y, sum_z = edge_sums(
                field(part, 0)[last:], field(part, 1)[last:], field(part, 2)[last:]
            )
            sums[part, 0] = sum_y[0]
            sums[part, 1] = sum_z[0]

    def warm_field(part, comp):
        return warm[part, 0, comp]

    def basis_field(index):
        return lambda part, comp: basis[index, part, comp]

    @pl.when(me == 0)
    def _():
        below[...] = jnp.zeros_like(below)

    @pl.when(me == n_space - 1)
    def _():
        above[...] = jnp.zeros_like(above)

    for part in range(2):
        sum_y, sum_z = edge_sums(*[warm[part, 0, c][last:] for c in range(3)])
        sums[0, part, 0] = sum_y[0]
        sums[0, part, 1] = sum_z[0]

    pl.semaphore_wait(barrier, n_space - 1 + n_src - 1)

    def halo_copies(step):
        first = warm.at[:, 0, pl.ds(1, 2), 0] if step == 0 else basis.at[step - 1, :, pl.ds(1, 2), 0]
        upward = pltpu.make_async_remote_copy(
            src_ref=sums.at[step],
            dst_ref=below.at[step],
            send_sem=halo_send.at[step, 0],
            recv_sem=halo_recv.at[step, 0],
            device_id={"space": lax.rem(me + 1, n_space)},
            device_id_type=MESH,
        )
        downward = pltpu.make_async_remote_copy(
            src_ref=first,
            dst_ref=above.at[step],
            send_sem=halo_send.at[step, 1],
            recv_sem=halo_recv.at[step, 1],
            device_id={"space": lax.rem(me + n_space - 1, n_space)},
            device_id_type=MESH,
        )
        return upward, downward

    def start_halo(step):
        upward, downward = halo_copies(step)

        @pl.when(me < n_space - 1)
        def _():
            upward.start()

        @pl.when(me > 0)
        def _():
            downward.start()

    def wait_halo(step):
        upward, downward = halo_copies(step)

        @pl.when(me > 0)
        def _():
            upward.wait_recv()

        @pl.when(me < n_space - 1)
        def _():
            downward.wait_recv()

    def end_halo(step):
        upward, downward = halo_copies(step)

        @pl.when(me < n_space - 1)
        def _():
            upward.wait_send()

        @pl.when(me > 0)
        def _():
            downward.wait_send()

    def measured_copy(off):
        return pltpu.make_async_remote_copy(
            src_ref=measured,
            dst_ref=measured_all.at[off],
            send_sem=measured_send.at[off],
            recv_sem=measured_recv.at[off],
            device_id={"space": lax.rem(me + off, n_space)},
            device_id_type=MESH,
        )

    def gram_copy(off):
        return pltpu.make_async_remote_copy(
            src_ref=gram_all.at[me],
            dst_ref=gram_all.at[me],
            send_sem=gram_send.at[off],
            recv_sem=gram_recv.at[off],
            device_id={"space": lax.rem(me + off, n_space)},
            device_id_type=MESH,
        )

    def gram_arrival(off):
        return pltpu.make_async_remote_copy(
            src_ref=gram_all.at[me],
            dst_ref=gram_all.at[lax.rem(me + n_space - off, n_space)],
            send_sem=gram_send.at[off],
            recv_sem=gram_recv.at[off],
            device_id={"space": lax.rem(me + off, n_space)},
            device_id_type=MESH,
        )

    def share_copy(off):
        peer = lax.rem(pair + off, n_src)
        return pltpu.make_async_remote_copy(
            src_ref=shares.at[peer],
            dst_ref=shares_in.at[off],
            send_sem=share_send.at[off],
            recv_sem=share_recv.at[off],
            device_id={"src": peer},
            device_id_type=MESH,
        )

    for off in range(1, n_space):
        measured_copy(off).start()
    start_halo(0)

    damping = wave_k * conductivity[...]

    for part in range(2):
        curled = curl_curl(*[warm[part, 0, c] for c in range(3)])
        for c in range(3):
            turned = damping * warm[1 - part, 0, c]
            basis[0, part, c] = -(curled[c] - turned if part == 0 else curled[c] + turned)

    for off in range(1, n_space):
        measured_copy(off).wait_recv()
    shift_z = rows_z.bit_length() - 1
    row_count = 3 * planes * rows_y
    sites = measured.shape[2]
    row_id = lax.broadcasted_iota(jnp.int32, (row_count, sites), 0)
    lane_id = lax.broadcasted_iota(jnp.int32, (rows_z, sites), 0)
    row_hot = []
    pieces = [[] for _ in range(6)]
    for off in range(n_space):
        sender = lax.rem(me + n_space - off, n_space)
        owner = layer[pl.ds(sender, 1), :]
        where_cell = cell[pl.ds(sender, 1), :]
        row = component[pl.ds(sender, 1), :] * (planes * rows_y) + lax.shift_right_logical(
            where_cell, shift_z
        )
        row = jnp.where(owner == me, row, -1)
        row_hot.append(jnp.where(row_id == row, 1.0, 0.0).astype(jnp.bfloat16))
        lane_hit = lane_id == jnp.bitwise_and(where_cell, rows_z - 1)
        for part in range(2):
            value = measured[part] if off == 0 else measured_all[off, part]
            rest = value
            for piece in range(3):
                rounded = rest.astype(jnp.bfloat16).astype(jnp.float32)
                rest = rest - rounded
                pieces[part * 3 + piece].append(
                    jnp.where(lane_hit, rounded, 0.0).astype(jnp.bfloat16)
                )
    hot = jnp.concatenate(row_hot, axis=1)
    for part in range(2):
        total = None
        for piece in range(3):
            term = lax.dot_general(
                hot,
                jnp.concatenate(pieces[part * 3 + piece], axis=1),
                (((1,), (1,)), ((), ())),
                preferred_element_type=jnp.float32,
            )
            total = term if total is None else total + term
        source[part] = total.reshape(3, planes, rows_y, rows_z)
    for part in range(2):
        for c in range(3):
            basis[0, part, c] = basis[0, part, c] + source[part, c]

    slots = gram_slots()
    cells = 3 * planes * rows_y

    def gram_column(k):
        for j in range(k + 1):
            left = [basis[j, part].reshape(cells, rows_z) for part in range(2)]
            right = [basis[k, part].reshape(cells, rows_z) for part in range(2)]
            spot = slots[j, k, 0]
            gram_rows[spot : spot + 1, :] = jnp.sum(
                left[0] * right[0] + left[1] * right[1], axis=0, keepdims=True
            )
            if j < k:
                spot = slots[j, k, 1]
                gram_rows[spot : spot + 1, :] = jnp.sum(
                    left[0] * right[1] - left[1] * right[0], axis=0, keepdims=True
                )

    def correct(step, sign):
        for part in range(2):
            over_y = sign * above[step, part, 0]
            over_z = sign * above[step, part, 1]
            slope = (over_y - down(over_y, 0, 0.0)) + (over_z - down(over_z, 1, 0.0))
            basis[step, part, 0, last] = basis[step, part, 0, last] + slope
            basis[step, part, 1, last] = basis[step, part, 1, last] - over_y
            basis[step, part, 2, last] = basis[step, part, 2, last] - over_z
            basis[step, part, 1, 0] = basis[step, part, 1, 0] - sign * below[step, part, 0]
            basis[step, part, 2, 0] = basis[step, part, 2, 0] - sign * below[step, part, 1]

    for k in range(ITERS + 1):
        wait_halo(k)
        correct(k, -1.0 if k == 0 else 1.0)
        if k < ITERS:
            for part in range(2):
                sum_y, sum_z = edge_sums(*[basis[k, part, c][last:] for c in range(3)])
                sums[k + 1, part, 0] = sum_y[0]
                sums[k + 1, part, 1] = sum_z[0]
            start_halo(k + 1)
            for part in range(2):
                curled = curl_curl(*[basis[k, part, c] for c in range(3)])
                for c in range(3):
                    turned = damping * basis[k, 1 - part, c]
                    moved = curled[c] - SHIFT * basis[k, part, c]
                    basis[k + 1, part, c] = moved - turned if part == 0 else moved + turned
        gram_column(k)

    count = len(slots)
    held = gram_rows.shape[0]
    lanes = lax.broadcasted_iota(jnp.int32, (held, rows_z), 1)
    rows = lax.broadcasted_iota(jnp.int32, (held, rows_z), 0)
    row_sums = jnp.sum(jnp.where(rows < count, gram_rows[...], 0.0), axis=1, keepdims=True)
    gram_all[me] = jnp.sum(jnp.where(lanes == rows, row_sums, 0.0), axis=0, keepdims=True)
    for off in range(1, n_space):
        gram_copy(off).start()
    for off in range(1, n_space):
        gram_arrival(off).wait_recv()
    total = gram_all[0]
    for index in range(1, n_space):
        total = total + gram_all[index]
    splat = {
        key: jnp.broadcast_to(total[:, spot : spot + 1], (8, rows_z)) for key, spot in slots.items()
    }

    def gram(j, k):
        real = splat[min(j, k), max(j, k), 0]
        if j == k:
            return real, jnp.zeros_like(real)
        imag = splat[min(j, k), max(j, k), 1]
        return real, imag if j < k else -imag

    update = combination(gram)

    local = None
    tiles = (planes * rows_y // 8, 8, rows_z)
    for c in range(3):
        real = warm[0, 0, c].reshape(tiles)
        imag = warm[1, 0, c].reshape(tiles)
        for k in range(ITERS):
            field_re = basis[k, 0, c].reshape(tiles)
            field_im = basis[k, 1, c].reshape(tiles)
            coef_re, coef_im = update[k][0][None], update[k][1][None]
            real = real + (coef_re * field_re - coef_im * field_im)
            imag = imag + (coef_re * field_im + coef_im * field_re)
        adjoint[0, 0, c] = real.reshape(planes, rows_y, rows_z)
        adjoint[1, 0, c] = imag.reshape(planes, rows_y, rows_z)
        term = real * background[1, 0, c].reshape(tiles) + imag * background[0, 0, c].reshape(tiles)
        local = term if local is None else local + term
    local = (wave_k * local).reshape(planes, rows_y, rows_z)
    share = rows_y // n_src
    for index in range(n_src):
        shares[index] = local[:, index * share : (index + 1) * share]
    for off in range(1, n_src):
        share_copy(off).start()
    for off in range(1, n_src):
        share_copy(off).wait_recv()
    result = shares[pair]
    for off in range(1, n_src):
        result = result + shares_in[off]
    gradient[...] = result

    for off in range(1, n_space):
        measured_copy(off).wait_send()
    for k in range(ITERS + 1):
        end_halo(k)
    for off in range(1, n_space):
        gram_copy(off).wait_send()
    for off in range(1, n_src):
        share_copy(off).wait_send()


def shards(
    n_space,
    n_src,
    background,
    warm_start,
    conductivity,
    frequencies,
    pair_freq,
    weighted_residual,
    datum_layer_index,
    receiver_flat_cell,
    receiver_component,
):
    planes, rows_y, rows_z = conductivity.shape
    sites = weighted_residual.shape[2]
    held = -(-len(gram_slots()) // 8) * 8
    vmem = pl.BlockSpec(memory_space=pltpu.VMEM)
    smem = pl.BlockSpec(memory_space=pltpu.SMEM)
    f32 = jnp.float32
    dma = pltpu.SemaphoreType.DMA
    return pl.pallas_call(
        functools.partial(kernel, n_space, n_src),
        out_shape=(
            jax.ShapeDtypeStruct(warm_start.shape, f32),
            jax.ShapeDtypeStruct((planes, rows_y // n_src, rows_z), f32),
        ),
        in_specs=[vmem, vmem, vmem, smem, smem, vmem, vmem, vmem, vmem],
        out_specs=(vmem, vmem),
        scratch_shapes=[
            pltpu.VMEM((ITERS + 1, 2, 3, planes, rows_y, rows_z), f32),
            pltpu.VMEM((ITERS + 1, 2, 2, rows_y, rows_z), f32),
            pltpu.VMEM((ITERS + 1, 2, 2, rows_y, rows_z), f32),
            pltpu.VMEM((ITERS + 1, 2, 2, rows_y, rows_z), f32),
            pltpu.VMEM((2, 3, planes, rows_y, rows_z), f32),
            pltpu.VMEM((n_space, 2, 1, sites), f32),
            pltpu.VMEM((held, rows_z), f32),
            pltpu.VMEM((n_space, 1, rows_z), f32),
            pltpu.VMEM((n_src, planes, rows_y // n_src, rows_z), f32),
            pltpu.VMEM((n_src, planes, rows_y // n_src, rows_z), f32),
            dma((ITERS + 1, 2)),
            dma((ITERS + 1, 2)),
            dma((n_space,)),
            dma((n_space,)),
            dma((n_space,)),
            dma((n_space,)),
            dma((n_src,)),
            dma((n_src,)),
        ],
        compiler_params=pltpu.CompilerParams(collective_id=0, has_side_effects=True),
    )(
        background,
        warm_start,
        conductivity,
        frequencies,
        pair_freq,
        weighted_residual,
        datum_layer_index.reshape(n_space, sites),
        receiver_flat_cell.reshape(n_space, sites),
        receiver_component.reshape(n_space, sites),
    )


def solution(mesh):
    placed = (
        P(None, "src", None, "space", None, None),
        P(None, "src", None, "space", None, None),
        P("space", None, None),
        P(),
        P("src"),
        P(None, "src", "space"),
        P(),
        P(),
        P(),
    )
    return jax.shard_map(
        functools.partial(shards, mesh.shape["space"], mesh.shape["src"]),
        mesh=mesh,
        in_specs=placed,
        out_specs=(P(None, "src", None, "space", None, None), P("space", "src", None)),
        check_vma=False,
    )
```

time: 211 us -> 35.7 us (0.17)
  blocking collectives: 62.3 us -> 0 us
  starting transfers between devices: 35.5 us -> 0 us
  between operations: 36.6 us -> 1.29 us
  waiting for transfers between devices: 33.2 us -> 0 us
  Pallas kernels: 0 us -> 32 us
  other arithmetic: 29.3 us -> 0 us
  local copies, waits for them, and re-layouts: 13.4 us -> 2.22 us
    psum x4 -> x0, blocking collectives: 62.3 us -> none  [the longest x3 47.2 us: shards(): lax.psum((fresh_re, fresh_im, squared(fresh), turn_re, turn_im), 'space')]
    pallas_call x0 -> x1, Pallas kernels: none -> 32 us  [shards(): pl.pallas_call(functools.partial(kernel, n_space, n_src), out_shape=(jax....]
    ppermute x10 -> x0, starting transfers between devices: 30.2 us -> none  [from_behind(): return lax.ppermute(block, axis, route)]
    reduce_scatter x1 -> x0, waiting for transfers between devices: 21.2 us -> none  [shards(): lax.psum_scatter(local_terms, 'src', scatter_dimension=1, tiled=True)]
    scatter-add x1 -> x0, other arithmetic: 14.6 us -> none  [shards(): jnp.zeros((2, pair_count, 3 * slab_cells), jnp.float32).at[:, :, target]]
    ppermute x10 -> x0, waiting for transfers between devices: 11.9 us -> none  [from_behind(): return lax.ppermute(block, axis, route)]
    reshape x1 -> x0, local copies, waits for them, and re-layouts: 7.59 us -> none  [shards(): source = flat_src.reshape(2, pair_count, 3, planes, rows_y, rows_z)]
    reduce_sum x7 -> x0, other arithmetic: 5.58 us -> none  [the longest x4 2.89 us: inner(): jnp.sum(first_vec[0] * second_vec[0] + first_vec[1] * second_vec[1], axis...]
  transfers between devices with their start and end apart: 12 -> 0, of which waited for: 8 -> 0; matrix products, arithmetic and copies ran while one was open for 14% -> 0% of each run, Pallas kernels for 0% -> 0%
where the time goes in v1:
time: 35.7 us; the launch traced here: 35.6 us
  Pallas kernels  32 us (90%)
  local copies, waits for them, and re-layouts  2.22 us (6%)
  between operations  1.29 us (4%)
    pallas_call x1, Pallas kernels, shards(): pl.pallas_call(functools.partial(kernel, n_space, n_src), out_shape=(jax....  32 us
    unnamed x4, local copies, waits for them, and re-layouts  2.22 us

profile of v1, /device:TPU:0, one launch (start us, length us, event | category | flops | bytes accessed | tf_op | source)
XLA Modules:
  0.0 35.6 jit_solution(4940052692629662805)
XLA Ops:
  1.3 32.0 %shard_map.104 = (f32[2,1,3,2,32,128]{5,4,3,2,1,0:T(8,128)}, f32[2,8,128]{2,1,0:T(8,128)}) custom-call(f32[2,1,3,2,32,128]{5,4,3,2,1,0:T(8,128)} %background.1, f32[2,1,3,2,32,128]{5,4,3,2,1,0:T(8,128)} %warm.1, f32[2,32,128]{2,1,0:T(8,128)} %conductivity.1, f32[8]{0:T(128)} %frequencies.1, s32[1]{0:T(128)S(6)} %copy.13.pair_freq, f32[2,1,128]{2,1,0:T(1,128)} %measured.1, ...), custom_call_target="tpu_custom_call" | custom-call | tf_op jit(solution)/shard_map/pallas_call | solution.py:466
  33.3 0.0 copy-start
  33.3 1.6 %copy.14 = f32[2,1,3,2,32,128]{5,4,3,2,1,0:T(8,128)} copy(f32[2,1,3,2,32,128]{5,4,3,2,1,0:T(8,128)} %get-tuple-element.4) | data formatting | bytes 393216
  35.0 0.0 copy-done
  35.0 0.6 %copy.15 = f32[2,8,128]{2,1,0:T(8,128)} copy(f32[2,8,128]{2,1,0:T(8,128)S(1)} %copy-done) | data formatting | bytes 16384
Async XLA Ops:
  33.3 1.6 %copy-start = (f32[2,8,128]{2,1,0:T(8,128)S(1)}, f32[2,8,128]{2,1,0:T(8,128)}, u32[]{:S(2)}) copy-start(f32[2,8,128]{2,1,0:T(8,128)} %get-tuple-element.5) | copy-start | bytes 24580

commit v2 on v1

--- a/solution.py
+++ b/solution.py
@@ -108,17 +108,26 @@
 def kernel(
     n_space,
     n_src,
+    background_hbm,
+    warm_hbm,
+    conductivity_hbm,
+    frequencies,
+    pair_freq,
+    measured_hbm,
+    layer_hbm,
+    cell_hbm,
+    component_hbm,
+    adjoint,
+    gradient,
     background,
     warm,
     conductivity,
-    frequencies,
-    pair_freq,
     measured,
     layer,
     cell,
     component,
-    adjoint,
-    gradient,
+    hot,
+    load_sem,
     basis,
     sums,
     above,
@@ -153,21 +162,24 @@
             barrier, 1, device_id={"src": lax.rem(pair + off, n_src)}, device_id_type=MESH
         )
 
+    loads = [
+        pltpu.make_async_copy(source_ref, target_ref, load_sem.at[index])
+        for index, (source_ref, target_ref) in enumerate(
+            [
+                (warm_hbm, warm),
+                (conductivity_hbm, conductivity),
+                (layer_hbm, layer),
+                (cell_hbm, cell),
+                (component_hbm, component),
+                (measured_hbm, measured),
+                (background_hbm, background),
+            ]
+        )
+    ]
+    for load in loads:
+        load.start()
+
     wave_k = frequencies[pair_freq[0]]
-
-    def store_sums(field):
-        for part in range(2):
-            sum_y, sum_z = edge_sums(
-                field(part, 0)[last:], field(part, 1)[last:], field(part, 2)[last:]
-            )
-            sums[part, 0] = sum_y[0]
-            sums[part, 1] = sum_z[0]
-
-    def warm_field(part, comp):
-        return warm[part, 0, comp]
-
-    def basis_field(index):
-        return lambda part, comp: basis[index, part, comp]
 
     @pl.when(me == 0)
     def _():
@@ -177,6 +189,7 @@
     def _():
         above[...] = jnp.zeros_like(above)
 
+    loads[0].wait()
     for part in range(2):
         sum_y, sum_z = edge_sums(*[warm[part, 0, c][last:] for c in range(3)])
         sums[0, part, 0] = sum_y[0]
@@ -185,7 +198,7 @@
     pl.semaphore_wait(barrier, n_space - 1 + n_src - 1)
 
     def halo_copies(step):
-        first = warm.at[:, 0, pl.ds(1, 2), 0] if step == 0 else basis.at[step - 1, :, pl.ds(1, 2), 0]
+        first = warm_hbm.at[:, 0, pl.ds(1, 2), 0] if step == 0 else basis.at[step - 1, :, pl.ds(1, 2), 0]
         upward = pltpu.make_async_remote_copy(
             src_ref=sums.at[step],
             dst_ref=below.at[step],
@@ -239,7 +252,7 @@
 
     def measured_copy(off):
         return pltpu.make_async_remote_copy(
-            src_ref=measured,
+            src_ref=measured_hbm,
             dst_ref=measured_all.at[off],
             send_sem=measured_send.at[off],
             recv_sem=measured_recv.at[off],
@@ -282,6 +295,8 @@
         measured_copy(off).start()
     start_halo(0)
 
+    for load in loads[1:6]:
+        load.wait()
     damping = wave_k * conductivity[...]
 
     for part in range(2):
@@ -290,45 +305,48 @@
             turned = damping * warm[1 - part, 0, c]
             basis[0, part, c] = -(curled[c] - turned if part == 0 else curled[c] + turned)
 
-    for off in range(1, n_space):
-        measured_copy(off).wait_recv()
     shift_z = rows_z.bit_length() - 1
     row_count = 3 * planes * rows_y
     sites = measured.shape[2]
     row_id = lax.broadcasted_iota(jnp.int32, (row_count, sites), 0)
     lane_id = lax.broadcasted_iota(jnp.int32, (rows_z, sites), 0)
-    row_hot = []
+
+    def sender(off):
+        return pl.ds(lax.rem(me + n_space - off, n_space), 1)
+
+    for off in range(n_space):
+        row = component[sender(off), :] * (planes * rows_y) + lax.shift_right_logical(
+            cell[sender(off), :], shift_z
+        )
+        row = jnp.where(layer[sender(off), :] == me, row, -1)
+        hot[:, off * sites : (off + 1) * sites] = jnp.where(row_id == row, 1.0, 0.0).astype(
+            jnp.bfloat16
+        )
+    for off in range(1, n_space):
+        measured_copy(off).wait_recv()
     pieces = [[] for _ in range(6)]
     for off in range(n_space):
-        sender = lax.rem(me + n_space - off, n_space)
-        owner = layer[pl.ds(sender, 1), :]
-        where_cell = cell[pl.ds(sender, 1), :]
-        row = component[pl.ds(sender, 1), :] * (planes * rows_y) + lax.shift_right_logical(
-            where_cell, shift_z
-        )
-        row = jnp.where(owner == me, row, -1)
-        row_hot.append(jnp.where(row_id == row, 1.0, 0.0).astype(jnp.bfloat16))
-        lane_hit = lane_id == jnp.bitwise_and(where_cell, rows_z - 1)
+        lane_hit = lane_id == jnp.bitwise_and(cell[sender(off), :], rows_z - 1)
         for part in range(2):
-            value = measured[part] if off == 0 else measured_all[off, part]
-            rest = value
+            rest = measured[part] if off == 0 else measured_all[off, part]
             for piece in range(3):
                 rounded = rest.astype(jnp.bfloat16).astype(jnp.float32)
                 rest = rest - rounded
                 pieces[part * 3 + piece].append(
                     jnp.where(lane_hit, rounded, 0.0).astype(jnp.bfloat16)
                 )
-    hot = jnp.concatenate(row_hot, axis=1)
+    placed = lax.dot_general(
+        hot[...],
+        jnp.concatenate([jnp.concatenate(block, axis=1) for block in pieces], axis=0),
+        (((1,), (1,)), ((), ())),
+        preferred_element_type=jnp.float32,
+    )
     for part in range(2):
-        total = None
-        for piece in range(3):
-            term = lax.dot_general(
-                hot,
-                jnp.concatenate(pieces[part * 3 + piece], axis=1),
-                (((1,), (1,)), ((), ())),
-                preferred_element_type=jnp.float32,
-            )
-            total = term if total is None else total + term
+        terms = [
+            placed[:, index * rows_z : (index + 1) * rows_z]
+            for index in range(part * 3, part * 3 + 3)
+        ]
+        total = (terms[0] + terms[1]) + terms[2]
         source[part] = total.reshape(3, planes, rows_y, rows_z)
     for part in range(2):
         for c in range(3):
@@ -404,6 +422,7 @@
         return real, imag if j < k else -imag
 
     update = combination(gram)
+    loads[6].wait()
 
     local = None
     tiles = (planes * rows_y // 8, 8, rows_z)
@@ -460,18 +479,28 @@
     sites = weighted_residual.shape[2]
     held = -(-len(gram_slots()) // 8) * 8
     vmem = pl.BlockSpec(memory_space=pltpu.VMEM)
+    hbm = pl.BlockSpec(memory_space=pltpu.HBM)
     smem = pl.BlockSpec(memory_space=pltpu.SMEM)
     f32 = jnp.float32
     dma = pltpu.SemaphoreType.DMA
     return pl.pallas_call(
         functools.partial(kernel, n_space, n_src),
         out_shape=(
-            jax.ShapeDtypeStruct(warm_start.shape, f32),
-            jax.ShapeDtypeStruct((planes, rows_y // n_src, rows_z), f32),
+            pltpu.VMEM(warm_start.shape, f32),
+            pltpu.VMEM((planes, rows_y // n_src, rows_z), f32),
         ),
-        in_specs=[vmem, vmem, vmem, smem, smem, vmem, vmem, vmem, vmem],
+        in_specs=[hbm, hbm, hbm, smem, smem, hbm, hbm, hbm, hbm],
         out_specs=(vmem, vmem),
         scratch_shapes=[
+            pltpu.VMEM(background.shape, f32),
+            pltpu.VMEM(warm_start.shape, f32),
+            pltpu.VMEM(conductivity.shape, f32),
+            pltpu.VMEM(weighted_residual.shape, f32),
+            pltpu.VMEM((n_space, sites), jnp.int32),
+            pltpu.VMEM((n_space, sites), jnp.int32),
+            pltpu.VMEM((n_space, sites), jnp.int32),
+            pltpu.VMEM((3 * planes * rows_y, n_space * sites), jnp.bfloat16),
+            dma((7,)),
             pltpu.VMEM((ITERS + 1, 2, 3, planes, rows_y, rows_z), f32),
             pltpu.VMEM((ITERS + 1, 2, 2, rows_y, rows_z), f32),
             pltpu.VMEM((ITERS + 1, 2, 2, rows_y, rows_z), f32),

time: 35.7 us -> 34.1 us (0.955)
  local copies, waits for them, and re-layouts: 2.22 us -> 1.28 us
  Pallas kernels: 32 us -> 31.4 us
    unnamed x4 -> x2, local copies, waits for them, and re-layouts: 2.22 us -> 1.28 us
    pallas_call x1, Pallas kernels: 32 us -> 31.4 us  [shards(): pl.pallas_call(functools.partial(kernel, n_space, n_src), out_shape=(pltp...]
where the time goes in v2:
time: 34.1 us; the launch traced here: 34 us
  Pallas kernels  31.4 us (92%)
  between operations  1.29 us (4%)
  local copies, waits for them, and re-layouts  1.28 us (4%)
    pallas_call x1, Pallas kernels, shards(): pl.pallas_call(functools.partial(kernel, n_space, n_src), out_shape=(pltp...  31.4 us
    unnamed x2, local copies, waits for them, and re-layouts  1.28 us

profile of v2, /device:TPU:0, one launch (start us, length us, event | category | flops | bytes accessed | tf_op | source)
XLA Modules:
  0.0 34.0 jit_solution(16178675916411042994)
XLA Ops:
  1.3 31.4 %shard_map.104 = (f32[2,1,3,2,32,128]{5,4,3,2,1,0:T(8,128)S(1)}, f32[2,8,128]{2,1,0:T(8,128)S(1)}) custom-call(f32[2,1,3,2,32,128]{5,4,3,2,1,0:T(8,128)} %background_hbm.1, f32[2,1,3,2,32,128]{5,4,3,2,1,0:T(8,128)} %warm_hbm.1, f32[2,32,128]{2,1,0:T(8,128)} %conductivity_hbm.1, f32[8]{0:T(128)} %frequencies.1, s32[1]{0:T(128)S(6)} %copy.15.pair_freq, ...), custom_call_target="tpu_custom_call" | custom-call | tf_op jit(solution)/shard_map/pallas_call | solution.py:486
  32.7 0.7 %copy.13 = f32[2,1,3,2,32,128]{5,4,3,2,1,0:T(8,128)} copy(f32[2,1,3,2,32,128]{5,4,3,2,1,0:T(8,128)S(1)} %get-tuple-element.2) | data formatting | bytes 393216
  33.4 0.6 %copy.14 = f32[2,8,128]{2,1,0:T(8,128)} copy(f32[2,8,128]{2,1,0:T(8,128)S(1)} %get-tuple-element.3) | data formatting | bytes 16384

commit v3 on v2

--- a/solution.py
+++ b/solution.py
@@ -54,6 +54,15 @@
     for term in terms[1:]:
         total = c_add(total, term)
     return total
+
+
+def flipped(index, mask):
+    result = index
+    for bit in range(mask.bit_length()):
+        if mask >> bit & 1:
+            place = 1 << bit
+            result = result + place - 2 * place * lax.rem(index // place, 2)
+    return result
 
 
 def gram_slots():
@@ -111,7 +120,7 @@
     background_hbm,
     warm_hbm,
     conductivity_hbm,
-    frequencies,
+    frequencies_hbm,
     pair_freq,
     measured_hbm,
     layer_hbm,
@@ -122,6 +131,7 @@
     background,
     warm,
     conductivity,
+    frequencies,
     measured,
     layer,
     cell,
@@ -173,13 +183,12 @@
                 (component_hbm, component),
                 (measured_hbm, measured),
                 (background_hbm, background),
+                (frequencies_hbm, frequencies),
             ]
         )
     ]
     for load in loads:
         load.start()
-
-    wave_k = frequencies[pair_freq[0]]
 
     @pl.when(me == 0)
     def _():
@@ -256,27 +265,17 @@
             dst_ref=measured_all.at[off],
             send_sem=measured_send.at[off],
             recv_sem=measured_recv.at[off],
-            device_id={"space": lax.rem(me + off, n_space)},
+            device_id={"space": flipped(me, off)},
             device_id_type=MESH,
         )
 
-    def gram_copy(off):
+    def gram_copy(mask):
         return pltpu.make_async_remote_copy(
-            src_ref=gram_all.at[me],
-            dst_ref=gram_all.at[me],
-            send_sem=gram_send.at[off],
-            recv_sem=gram_recv.at[off],
-            device_id={"space": lax.rem(me + off, n_space)},
-            device_id_type=MESH,
-        )
-
-    def gram_arrival(off):
-        return pltpu.make_async_remote_copy(
-            src_ref=gram_all.at[me],
-            dst_ref=gram_all.at[lax.rem(me + n_space - off, n_space)],
-            send_sem=gram_send.at[off],
-            recv_sem=gram_recv.at[off],
-            device_id={"space": lax.rem(me + off, n_space)},
+            src_ref=gram_all.at[0],
+            dst_ref=gram_all.at[mask],
+            send_sem=gram_send.at[mask],
+            recv_sem=gram_recv.at[mask],
+            device_id={"space": flipped(me, mask)},
             device_id_type=MESH,
         )
 
@@ -291,12 +290,13 @@
             device_id_type=MESH,
         )
 
-    for off in range(1, n_space):
+    for off in range(n_space - 1, 0, -1):
         measured_copy(off).start()
     start_halo(0)
 
-    for load in loads[1:6]:
+    for load in loads[1:6] + loads[7:]:
         load.wait()
+    wave_k = frequencies[pair_freq[0]]
     damping = wave_k * conductivity[...]
 
     for part in range(2):
@@ -312,7 +312,7 @@
     lane_id = lax.broadcasted_iota(jnp.int32, (rows_z, sites), 0)
 
     def sender(off):
-        return pl.ds(lax.rem(me + n_space - off, n_space), 1)
+        return pl.ds(flipped(me, off), 1)
 
     for off in range(n_space):
         row = component[sender(off), :] * (planes * rows_y) + lax.shift_right_logical(
@@ -402,14 +402,16 @@
     lanes = lax.broadcasted_iota(jnp.int32, (held, rows_z), 1)
     rows = lax.broadcasted_iota(jnp.int32, (held, rows_z), 0)
     row_sums = jnp.sum(jnp.where(rows < count, gram_rows[...], 0.0), axis=1, keepdims=True)
-    gram_all[me] = jnp.sum(jnp.where(lanes == rows, row_sums, 0.0), axis=0, keepdims=True)
-    for off in range(1, n_space):
-        gram_copy(off).start()
-    for off in range(1, n_space):
-        gram_arrival(off).wait_recv()
-    total = gram_all[0]
-    for index in range(1, n_space):
-        total = total + gram_all[index]
+    gram_all[0] = jnp.sum(jnp.where(lanes == rows, row_sums, 0.0), axis=0, keepdims=True)
+    gram_copies = [gram_copy(mask) for mask in range(n_space - 1, 0, -1)]
+    for copy in gram_copies:
+        copy.start()
+    for copy in gram_copies:
+        copy.wait_recv()
+    level = [gram_all[mask] for mask in range(n_space)]
+    while len(level) > 1:
+        level = [level[i] + level[i + 1] for i in range(0, len(level), 2)]
+    total = level[0]
     splat = {
         key: jnp.broadcast_to(total[:, spot : spot + 1], (8, rows_z)) for key, spot in slots.items()
     }
@@ -456,10 +458,21 @@
         measured_copy(off).wait_send()
     for k in range(ITERS + 1):
         end_halo(k)
-    for off in range(1, n_space):
-        gram_copy(off).wait_send()
+    for copy in gram_copies:
+        copy.wait_send()
     for off in range(1, n_src):
         share_copy(off).wait_send()
+
+
+def write_out(adjoint, gradient, adjoint_out, gradient_out, sems):
+    copies = [
+        pltpu.make_async_copy(adjoint, adjoint_out, sems.at[0]),
+        pltpu.make_async_copy(gradient, gradient_out, sems.at[1]),
+    ]
+    for copy in copies:
+        copy.start()
+    for copy in copies:
+        copy.wait()
 
 
 def shards(
@@ -480,27 +493,27 @@
     held = -(-len(gram_slots()) // 8) * 8
     vmem = pl.BlockSpec(memory_space=pltpu.VMEM)
     hbm = pl.BlockSpec(memory_space=pltpu.HBM)
-    smem = pl.BlockSpec(memory_space=pltpu.SMEM)
     f32 = jnp.float32
     dma = pltpu.SemaphoreType.DMA
-    return pl.pallas_call(
+    results = pl.pallas_call(
         functools.partial(kernel, n_space, n_src),
         out_shape=(
             pltpu.VMEM(warm_start.shape, f32),
             pltpu.VMEM((planes, rows_y // n_src, rows_z), f32),
         ),
-        in_specs=[hbm, hbm, hbm, smem, smem, hbm, hbm, hbm, hbm],
+        in_specs=[hbm] * 4 + [pl.BlockSpec(memory_space=pltpu.SMEM)] + [hbm] * 4,
         out_specs=(vmem, vmem),
         scratch_shapes=[
             pltpu.VMEM(background.shape, f32),
             pltpu.VMEM(warm_start.shape, f32),
             pltpu.VMEM(conductivity.shape, f32),
+            pltpu.SMEM(frequencies.shape, f32),
             pltpu.VMEM(weighted_residual.shape, f32),
             pltpu.VMEM((n_space, sites), jnp.int32),
             pltpu.VMEM((n_space, sites), jnp.int32),
             pltpu.VMEM((n_space, sites), jnp.int32),
             pltpu.VMEM((3 * planes * rows_y, n_space * sites), jnp.bfloat16),
-            dma((7,)),
+            dma((8,)),
             pltpu.VMEM((ITERS + 1, 2, 3, planes, rows_y, rows_z), f32),
             pltpu.VMEM((ITERS + 1, 2, 2, rows_y, rows_z), f32),
             pltpu.VMEM((ITERS + 1, 2, 2, rows_y, rows_z), f32),
@@ -533,6 +546,17 @@
         receiver_component.reshape(n_space, sites),
     )
 
+    return pl.pallas_call(
+        write_out,
+        out_shape=(
+            jax.ShapeDtypeStruct(warm_start.shape, f32),
+            jax.ShapeDtypeStruct((planes, rows_y // n_src, rows_z), f32),
+        ),
+        in_specs=[vmem] * 2,
+        out_specs=(hbm, hbm),
+        scratch_shapes=[dma((2,))],
+    )(*[pltpu.with_memory_space_constraint(result, pltpu.VMEM) for result in results])
+
 
 def solution(mesh):
     placed = (

time: 34.1 us -> 32.6 us (0.956)
  local copies, waits for them, and re-layouts: 1.28 us -> 0 us
    unnamed x2 -> x0, local copies, waits for them, and re-layouts: 1.28 us -> none
    pallas_call x1, Pallas kernels: 31.4 us -> 30.5 us  [shards(): pl.pallas_call(functools.partial(kernel, n_space, n_src), out_shape=(pltp...]
    pallas_call x0 -> x1, Pallas kernels: none -> 0.7 us  [shards(): pl.pallas_call(write_out, out_shape=(jax.ShapeDtypeStruct(warm_start.shap...]
where the time goes in v3:
time: 32.6 us; the launch traced here: 32.5 us
  Pallas kernels  31.2 us (96%)
  between operations  1.29 us (4%)
    pallas_call x1, Pallas kernels, shards(): pl.pallas_call(functools.partial(kernel, n_space, n_src), out_shape=(pltp...  30.5 us
    pallas_call x1, Pallas kernels, shards(): pl.pallas_call(write_out, out_shape=(jax.ShapeDtypeStruct(warm_start.shap...  0.7 us

profile of v3, /device:TPU:0, one launch (start us, length us, event | category | flops | bytes accessed | tf_op | source)
XLA Modules:
  0.0 32.5 jit_solution(6993706565740610155)
XLA Ops:
  1.3 30.5 %shard_map.104 = (f32[2,1,3,2,32,128]{5,4,3,2,1,0:T(8,128)S(1)}, f32[2,8,128]{2,1,0:T(8,128)S(1)}) custom-call(f32[2,1,3,2,32,128]{5,4,3,2,1,0:T(8,128)} %background_hbm.1, f32[2,1,3,2,32,128]{5,4,3,2,1,0:T(8,128)} %warm_hbm.1, f32[2,32,128]{2,1,0:T(8,128)} %conductivity_hbm.1, f32[8]{0:T(128)} %frequencies_hbm.1, s32[1]{0:T(128)S(6)} %copy.11.pair_freq, ...), custom_call_target="tpu_custom_call" | custom-call | tf_op jit(solution)/shard_map/pallas_call | solution.py:498
  31.8 0.7 %shard_map.105 = (f32[2,1,3,2,32,128]{5,4,3,2,1,0:T(8,128)}, f32[2,8,128]{2,1,0:T(8,128)}) custom-call(f32[2,1,3,2,32,128]{5,4,3,2,1,0:T(8,128)S(1)} %get-tuple-element.4.adjoint, f32[2,8,128]{2,1,0:T(8,128)S(1)} %get-tuple-element.5.gradient), custom_call_target="tpu_custom_call" | custom-call | tf_op jit(solution)/shard_map/pallas_call | solution.py:549
